TPU v7x, 32 devices: a whole 2x2x4 slice. The times are simulated.
32 devices in a mesh: groups: 2 (over y), req: 8 (over z, core), head: 2 (over x), rep: 1.
Axes of the slice: x: 2, y: 2, z: 4, core: 2. Of those that a mesh axis runs over, the one named last changes fastest.
Arguments:
- candidates: bfloat16 [32768, 1024], P(('groups', 'req', 'rep')), parts along dimension 0, may hold values from -6 to 6
- candidate_request: int32 [16, 2048], P(('groups', 'req'), 'rep'), parts along dimension 0, may hold values from 0 to 7, never falling along the last dimension, each value on 1 to 512 neighbouring positions
- request_owner: int32 [128, 1], P(('groups', 'req')), parts along dimension 0, may hold values from 0 to 7; in each aligned block of 8 rows (0 to 7, 8 to 15, ...) no two rows name the same one
- request_user: int32 [128], P(('groups', 'req')), parts along dimension 0, may hold values from 0 to 7
- request_blocks: int32 [16, 8], P(('groups', 'req')), parts along dimension 0, may hold values from 1 to 4, 24 in all within a row
- kv_cache: bfloat16 [128, 512, 2048], P(('groups', 'req'), None, 'head'), parts along dimension 0, may hold values from -6 to 6
- w_in: bfloat16 [1024, 4096], P(None, 'head'), may hold values from -0.1875 to 0.1875
- w_out: bfloat16 [1024, 1024], P('head'), may hold values from -0.1875 to 0.1875
Outputs:
- ranked: bfloat16 [32768, 1024], P(('groups', 'req', 'rep'), 'head'), parts along dimension 0
There are 2 independent parts, one for each index of `groups`. A program takes and returns all parts, laid end to end along the dimension named above; an argument that names none is the same for every part. Nothing has to cross between parts.
Inputs may be any that keep to these rules, and one draw needn't show every extreme that they name: `request_owner`: among the 8 requests of one req index at most 1 name the same owner, a bound that some block reaches of them. `request_blocks`: the 8 lengths of one req index sum to 24; some request has 4. `candidate_request`: never falls along the 2048 candidates of one req index; every request has 1 to 512 candidates, one exactly 512.
All inputs are finite; a program needn't handle non-finite values.
Results may differ from a plain program's by a relative error of at most 0.0056.
Values may be sent and summed in bfloat16 or wider, within the bound.
A program may use at most 128 MiB of HBM per device.

v0:
```python
import math
import jax
import jax.numpy as jnp
from jax import lax
from jax.sharding import PartitionSpec as P

HD = 128
BLOCK = 128
CAP = 1
MOSTC = 512
EPSILON = 1e-05


def normalize(values):
    center = values - jnp.mean(values, axis=-1, keepdims=True)
    spread = jnp.mean(center * center, axis=-1, keepdims=True)
    return center * lax.rsqrt(spread + EPSILON)


def slot_ranks(owner_rows):
    width = owner_rows.shape[-1]
    same_owner = owner_rows[..., :, None] == owner_rows[..., None, :]
    earlier = jnp.arange(width)[None, :] < jnp.arange(width)[:, None]
    return jnp.sum(jnp.logical_and(same_owner, earlier).astype(jnp.int32), axis=-1)


def per_device(
    candidates,
    candidate_request,
    request_owner,
    request_user,
    request_blocks,
    kv_cache,
    w_in,
    w_out,
):
    shard_rows = candidates.shape[0]
    local_heads = w_out.shape[0] // HD
    req_count = lax.axis_size("req")
    myself = lax.axis_index("req")
    owners = request_owner[:, 0]
    lengths = request_blocks[0]
    all_owners, all_users = (
        lax.all_gather(owners, "req", axis=0, tiled=True),
        lax.all_gather(request_user, "req", axis=0, tiled=True),
    )
    all_owners = all_owners.reshape(req_count, -1)
    all_users = all_users.reshape(req_count, -1)
    ranks_all = slot_ranks(all_owners)
    slot_ids = jnp.arange(CAP)
    chosen = jnp.logical_and(
        (all_owners == myself)[:, None, :], ranks_all[:, None, :] == slot_ids[None, :, None]
    )
    chosen_int = chosen.astype(jnp.int32)
    present = jnp.sum(chosen_int, axis=-1) > 0
    user_slot = jnp.sum(chosen_int * all_users[:, None, :], axis=-1)
    picked = kv_cache[user_slot]
    arrived = lax.all_to_all(
        jnp.where(present[:, :, None, None], picked, jnp.zeros_like(picked)),
        "req",
        split_axis=0,
        concat_axis=0,
        tiled=True,
    )
    own_ranks = slot_ranks(owners)
    normed = normalize(candidates.astype(jnp.float32)).astype(jnp.bfloat16)
    projected = jax.nn.silu(jnp.dot(normed, w_in, preferred_element_type=jnp.float32)).astype(
        jnp.bfloat16
    )
    projected = projected.reshape(shard_rows, local_heads, 4, HD)
    gates = projected[:, :, 0]
    values_own = projected[:, :, 1]
    queries = projected[:, :, 2]
    keys_own = projected[:, :, 3]
    scale = 1.0 / math.sqrt(HD)
    self_score = (
        jnp.sum(queries.astype(jnp.float32) * keys_own.astype(jnp.float32), axis=-1) * scale
    )
    attended = jax.nn.silu(self_score)[..., None] * values_own.astype(jnp.float32)
    segment = candidate_request[0]
    window = min(MOSTC, shard_rows)
    token_pos = jnp.arange(arrived.shape[2])

    def add_request(request, total):
        start = jnp.sum((segment < request).astype(jnp.int32))
        start = jnp.clip(start, 0, shard_rows - window)
        rows_q = lax.dynamic_slice_in_dim(queries, start, window, 0)
        rows_seg = lax.dynamic_slice_in_dim(segment, start, window, 0)
        source = owners[request]
        slot = own_ranks[request]
        cached = arrived[source, slot].reshape(-1, local_heads, 2, HD)
        live = token_pos < lengths[request] * BLOCK
        scores = (
            jnp.einsum("whd,thd->hwt", rows_q, cached[:, :, 0], preferred_element_type=jnp.float32)
            * scale
        )
        weights = jnp.where(live[None, None, :], jax.nn.silu(scores), 0.0).astype(jnp.bfloat16)
        mixed = jnp.einsum(
            "hwt,thd->whd", weights, cached[:, :, 1], preferred_element_type=jnp.float32
        )
        mixed = jnp.where((rows_seg == request)[:, None, None], mixed, 0.0)
        current = lax.dynamic_slice_in_dim(total, start, window, 0)
        return lax.dynamic_update_slice_in_dim(total, current + mixed, start, 0)

    attended = lax.fori_loop(0, owners.shape[0], add_request, attended)
    gated = (
        (normalize(attended) * gates.astype(jnp.float32))
        .astype(jnp.bfloat16)
        .reshape(shard_rows, -1)
    )
    partial_out = jnp.dot(gated, w_out, preferred_element_type=jnp.float32)
    summed = lax.psum_scatter(partial_out, "head", scatter_dimension=1, tiled=True)
    columns = summed.shape[1]
    residual = lax.dynamic_slice_in_dim(
        candidates, lax.axis_index("head") * columns, columns, 1
    ).astype(jnp.float32)
    return (summed + residual).astype(jnp.bfloat16)


def solution(mesh):
    placed = (
        P(("groups", "req", "rep"), None),
        P(("groups", "req"), "rep"),
        P(("groups", "req"), None),
        P(("groups", "req")),
        P(("groups", "req"), None),
        P(("groups", "req"), None, "head"),
        P(None, "head"),
        P("head", None),
    )
    return jax.shard_map(
        per_device,
        mesh=mesh,
        in_specs=placed,
        out_specs=P(("groups", "req", "rep"), "head"),
        check_vma=False,
    )
```

profile of v0, /device:TPU:0, one launch (start us, length us, event | category | flops | bytes accessed | tf_op | source)
XLA Modules:
  0.0 481.6 jit_solution(14917906185347774815)
XLA Ops:
  10.1 10.6 %all-reduce.2 = (s32[64]{0:T(128)S(1)}, s32[64]{0:T(128)S(1)}) all-reduce(s32[64]{0:T(128)S(1)} %bitcast_dynamic-update-slice_fusion, s32[64]{0:T(128)S(1)} %dynamic-update-slice.1), channel_id=2, replica_groups=mesh['groups'=2,'req'=8,'head'=2,'rep'=1] {'req'}, use_global_device_ids=true, to_apply=%add | all-reduce | flops 128 | bytes 1024
  21.5 8.1 %gather_fusion = bf16[8,512,1024]{2,1,0:T(8,128)(2,1)} fusion(bf16[8,512,1024]{2,1,0:T(8,128)(2,1)} %param.15, s32[1024]{0:T(1024)S(1)} %pad_clamp_fusion), kind=kCustom, calls=%fused_computation | custom fusion | bytes 16777248 | tf_op jit(solution)/shard_map/gather | solution.py:57
  29.6 7.2 %fusion.17 = bf16[8,1,512,1024]{3,2,1,0:T(8,128)(2,1)} fusion(bf16[8,512,1024]{2,1,0:T(8,128)(2,1)} %gather_fusion, pred[8]{0:T(512)(128)(4,1)S(1)} %broadcast_compare_fusion.1), kind=kLoop, calls=%fused_computation.26 | loop fusion | flops 4194304 | bytes 16777224 | tf_op jit(solution)/shard_map/jit(_where)/select_n | solution.py:59
  36.8 5.0 %all-to-all-start = ((bf16[8,1,512,1024]{3,2,1,0:T(8,128)(2,1)}), bf16[8,1,512,1024]{3,2,1,0:T(8,128)(2,1)}, u32[]{:S(2)}, u32[]{:S(2)}) async-start(bf16[8,1,512,1024]{3,2,1,0:T(8,128)(2,1)} %fusion.17), calls=%async_computation | async-start | bytes 16777216 | tf_op jit(solution)/shard_map/all_to_all | solution.py:58
  42.1 3.0 convert_reduce_fusion.1
  46.9 15.4 %multiply_convert_fusion = bf16[2048,2048]{0,1:T(8,128)(2,1)S(1)} fusion(bf16[1024,2048]{1,0:T(8,128)(2,1)} %param.16, bf16[2048,1024]{1,0:T(8,128)(2,1)S(1)} %copy-done.2, f32[2048]{0:T(1024)S(1)} %add_rsqrt_fusion.1, f32[2048]{0:T(1024)S(1)} %broadcast_multiply_fusion.1), kind=kOutput, calls=%fused_computation.18 | convolution fusion | flops 8619294720 | bytes 16793600 | tf_op jit(solution)/shard_map/dot_general | solution.py:67
  66.2 2.5 copy.46
  68.7 3.0 copy.47
  71.8 2.8 fusion.21
  74.6 4.2 convert_multiply_fusion.1
  78.7 146.9 %all-to-all-done = bf16[8,1,512,1024]{3,2,1,0:T(8,128)(2,1)} async-done(((bf16[8,1,512,1024]{3,2,1,0:T(8,128)(2,1)}), bf16[8,1,512,1024]{3,2,1,0:T(8,128)(2,1)}, u32[]{:S(2)}, u32[]{:S(2)}) %all-to-all-start) | async-done | bytes 8388640 | tf_op jit(solution)/shard_map/all_to_all | solution.py:58
  225.7 130.5 %while.14 = (s32[]{:T(128)}, f32[2048,4,128]{0,2,1:T(8,128)}, s32[2048]{0:T(1024)S(1)}, s32[8]{0:T(128)S(1)}, bf16[8,1,512,1024]{3,2,1,0:T(8,128)(2,1)}, /*index...) while((s32[]{:T(128)}, f32[2048,4,128]{0,2,1:T(8,128)}, ...), condition=%wide.region_8.9_spmd.clone, body=%wide.region_6.8_spmd.clone.sunk | while | flops 544742400 | bytes 9975023 | solution.py:105
  232.7 3.4 fusion.35
  236.2 5.8 %dynamic_update_slice.9 = f32[2048,4,128]{0,2,1:T(8,128)} dynamic-update-slice(f32[2048,4,128]{0,2,1:T(8,128)} %get-tuple-element.275, f32[512,4,128]{0,2,1:T(8,128)S(1)} %fusion.35, s32[]{:T(128)S(6)} %min.10, s32[]{:T(128)} %constant.90.clone.1..sunk, s32[]{:T(128)} %constant.90.clone.1..sunk) | dynamic-update-slice | bytes 2097156 | tf_op jit(solution)/shard_map/while/body/eval_jaxpr/dynamic_update_slice | solution.py:103
  248.9 3.4 fusion.35
  252.4 6.3 %dynamic_update_slice.9 = f32[2048,4,128]{0,2,1:T(8,128)} dynamic-update-slice(f32[2048,4,128]{0,2,1:T(8,128)} %get-tuple-element.275, f32[512,4,128]{0,2,1:T(8,128)S(1)} %fusion.35, s32[]{:T(128)S(6)} %min.10, s32[]{:T(128)} %constant.90.clone.1..sunk, s32[]{:T(128)} %constant.90.clone.1..sunk) | dynamic-update-slice | bytes 2097156 | tf_op jit(solution)/shard_map/while/body/eval_jaxpr/dynamic_update_slice | solution.py:103
  265.7 3.4 fusion.35
  269.1 6.3 %dynamic_update_slice.9 = f32[2048,4,128]{0,2,1:T(8,128)} dynamic-update-slice(f32[2048,4,128]{0,2,1:T(8,128)} %get-tuple-element.275, f32[512,4,128]{0,2,1:T(8,128)S(1)} %fusion.35, s32[]{:T(128)S(6)} %min.10, s32[]{:T(128)} %constant.90.clone.1..sunk, s32[]{:T(128)} %constant.90.clone.1..sunk) | dynamic-update-slice | bytes 2097156 | tf_op jit(solution)/shard_map/while/body/eval_jaxpr/dynamic_update_slice | solution.py:103
  282.4 3.4 fusion.35
  285.8 6.3 %dynamic_update_slice.9 = f32[2048,4,128]{0,2,1:T(8,128)} dynamic-update-slice(f32[2048,4,128]{0,2,1:T(8,128)} %get-tuple-element.275, f32[512,4,128]{0,2,1:T(8,128)S(1)} %fusion.35, s32[]{:T(128)S(6)} %min.10, s32[]{:T(128)} %constant.90.clone.1..sunk, s32[]{:T(128)} %constant.90.clone.1..sunk) | dynamic-update-slice | bytes 2097156 | tf_op jit(solution)/shard_map/while/body/eval_jaxpr/dynamic_update_slice | solution.py:103
  299.1 3.4 fusion.35
  302.6 6.3 %dynamic_update_slice.9 = f32[2048,4,128]{0,2,1:T(8,128)} dynamic-update-slice(f32[2048,4,128]{0,2,1:T(8,128)} %get-tuple-element.275, f32[512,4,128]{0,2,1:T(8,128)S(1)} %fusion.35, s32[]{:T(128)S(6)} %min.10, s32[]{:T(128)} %constant.90.clone.1..sunk, s32[]{:T(128)} %constant.90.clone.1..sunk) | dynamic-update-slice | bytes 2097156 | tf_op jit(solution)/shard_map/while/body/eval_jaxpr/dynamic_update_slice | solution.py:103
  315.8 3.4 fusion.35
  319.3 6.3 %dynamic_update_slice.9 = f32[2048,4,128]{0,2,1:T(8,128)} dynamic-update-slice(f32[2048,4,128]{0,2,1:T(8,128)} %get-tuple-element.275, f32[512,4,128]{0,2,1:T(8,128)S(1)} %fusion.35, s32[]{:T(128)S(6)} %min.10, s32[]{:T(128)} %constant.90.clone.1..sunk, s32[]{:T(128)} %constant.90.clone.1..sunk) | dynamic-update-slice | bytes 2097156 | tf_op jit(solution)/shard_map/while/body/eval_jaxpr/dynamic_update_slice | solution.py:103
  332.5 3.4 fusion.35
  335.9 5.0 %dynamic_update_slice.9 = f32[2048,4,128]{0,2,1:T(8,128)} dynamic-update-slice(f32[2048,4,128]{0,2,1:T(8,128)} %get-tuple-element.275, f32[512,4,128]{0,2,1:T(8,128)S(1)} %fusion.35, s32[]{:T(128)S(6)} %min.10, s32[]{:T(128)} %constant.90.clone.1..sunk, s32[]{:T(128)} %constant.90.clone.1..sunk) | dynamic-update-slice | bytes 2097156 | tf_op jit(solution)/shard_map/while/body/eval_jaxpr/dynamic_update_slice | solution.py:103
  347.8 3.3 fusion.35
  351.2 5.0 %dynamic_update_slice.9 = f32[2048,4,128]{0,2,1:T(8,128)} dynamic-update-slice(f32[2048,4,128]{0,2,1:T(8,128)} %get-tuple-element.275, f32[512,4,128]{0,2,1:T(8,128)S(1)} %fusion.35, s32[]{:T(128)S(6)} %min.10, s32[]{:T(128)} %constant.90.clone.1..sunk, s32[]{:T(128)} %constant.90.clone.1..sunk) | dynamic-update-slice | bytes 2097156 | tf_op jit(solution)/shard_map/while/body/eval_jaxpr/dynamic_update_slice | solution.py:103
  358.7 2.9 multiply_reduce_fusion
  364.6 5.6 %fusion.28 = f32[2048,1024]{1,0:T(8,128)} fusion(bf16[2048,512]{0,1:T(8,128)(2,1)S(1)} %bitcast.74, bf16[512,1024]{1,0:T(8,128)(2,1)S(1)} %copy-done), kind=kOutput, calls=%fused_computation.56 | convolution fusion | flops 2147483648 | bytes 11534336 | tf_op jit(solution)/shard_map/dot_general | solution.py:111
  370.2 99.7 %reduce-scatter.2.cloned.1.call-done = f32[2048,512]{1,0:T(8,128)} async-done(((f32[2048,1024]{1,0:T(8,128)}), f32[2048,512]{1,0:T(8,128)}) %reduce-scatter.2.cloned.1.call-update) | async-done | bytes 4194320 | tf_op jit(solution)/shard_map/reduce_scatter | solution.py:112
  469.9 4.9 %add_convert_fusion = bf16[2048,512]{1,0:T(8,128)(2,1)} fusion(f32[2048,512]{1,0:T(8,128)} %reduce-scatter.2.cloned.1.call-done, bf16[2048,1024]{1,0:T(8,128)(2,1)} %param.10, s32[]{:T(128)S(6)} %select_n.71), kind=kLoop, calls=%fused_computation.33 | loop fusion | flops 3145728 | bytes 8388612 | tf_op jit(solution)/shard_map/convert_element_type | solution.py:117
  (88 shorter events, 44.9 us)
Async XLA Ops:
  6.5 358.0 %copy-start = (bf16[512,1024]{1,0:T(8,128)(2,1)S(1)}, bf16[512,1024]{1,0:T(8,128)(2,1)}, u32[]{:S(2)}) copy-start(bf16[512,1024]{1,0:T(8,128)(2,1)} %param.17) | copy-start | bytes 3145732
  36.8 188.9 %all-to-all-start = ((bf16[8,1,512,1024]{3,2,1,0:T(8,128)(2,1)}), bf16[8,1,512,1024]{3,2,1,0:T(8,128)(2,1)}, u32[]{:S(2)}, u32[]{:S(2)}) async-start(bf16[8,1,512,1024]{3,2,1,0:T(8,128)(2,1)} %fusion.17), calls=%async_computation | async-start | bytes 16777216 | tf_op jit(solution)/shard_map/all_to_all | solution.py:58
  41.8 428.0 %reduce-scatter.2.cloned.1.call-start = ((), (), s32[]{:S(2)}) async-start(), calls=%async_computation.2 | async-start | bytes 12582912 | tf_op jit(solution)/shard_map/reduce_scatter | solution.py:112
  42.1 3.5 copy-start.2
  62.4 3.8 copy-start.3
  74.5 151.2 %copy-start.4 = (s32[1,2048]{1,0:T(1,128)S(1)}, s32[1,2048]{1,0:T(1,128)}, u32[]{:S(2)}) copy-start(s32[1,2048]{1,0:T(1,128)} %param.11) | copy-start | bytes 24580
  74.5 151.2 %copy-start.5 = (s32[8,1]{0,1:T(1,128)S(1)}, s32[8,1]{0,1:T(1,128)}, u32[]{:S(2)}) copy-start(s32[8,1]{0,1:T(1,128)} %param.12) | copy-start | bytes 100
  74.5 151.1 %copy-start.6 = (s32[1,8]{1,0:T(1,128)S(1)}, s32[1,8]{1,0:T(1,128)}, u32[]{:S(2)}) copy-start(s32[1,8]{1,0:T(1,128)} %param.14) | copy-start | bytes 100
  358.7 3.5 copy-start.1
Sparse Core Ops, SparseCore 0:
  370.3 99.4 reduce-scatter.1
where the time goes:
time: 484 us; the launch traced here: 482 us
  waiting for transfers between devices  247 us (51%)
  local copies, waits for them, and re-layouts  92.8 us (19%)
  matrix products  48.4 us (10%)
  other arithmetic  37.5 us (8%)
  loops' own time  26.2 us (5%)
  between operations  14.2 us (3%)
  blocking collectives  10.6 us (2%)
  starting transfers between devices  5.26 us (1%)
    all_to_all x1, waiting for transfers between devices, per_device(): lax.all_to_all(jnp.where(present[:, :, None, None], picked, jnp.zeros_lik...  147 us
    reduce_scatter x1, waiting for transfers between devices, per_device(): lax.psum_scatter(partial_out, 'head', scatter_dimension=1, tiled=True)  99.7 us
    dynamic_update_slice x8, local copies, waits for them, and re-layouts, add_request(): return lax.dynamic_update_slice_in_dim(total, current + mixed, start, 0)  47.1 us
    dot_general x8, matrix products, add_request(): jnp.einsum('hwt,thd->whd', weights, cached[:, :, 1], preferred_element_ty...  27.4 us
    another operation x1, loops' own time, per_device(): attended = lax.fori_loop(0, owners.shape[0], add_request, attended)  26.2 us
    dot_general x1, matrix products, per_device(): jnp.dot(normed, w_in, preferred_element_type=jnp.float32)  15.4 us
    dynamic_slice x16, local copies, waits for them, and re-layouts, add_request(): cached = arrived[source, slot].reshape(-1, local_heads, 2, HD)  14.7 us
    unnamed x21, local copies, waits for them, and re-layouts  11.2 us
  transfers between devices with their start and end apart: 2, of which 2 were waited for; matrix products, arithmetic and copies ran while one was open for 7% of the time, Pallas kernels for 0%

commit v1 on v0

--- a/solution.py
+++ b/solution.py
@@ -9,6 +9,18 @@
 CAP = 1
 MOSTC = 512
 EPSILON = 1e-05
+
+
+def split_up(value, dim, length):
+    shape = value.shape
+    blocks = value.reshape(*shape[:dim], length, shape[dim] // length, *shape[dim + 1 :])
+    return jnp.moveaxis(blocks, dim, 0)
+
+
+def joined_along(blocks, dim):
+    lengths = list(blocks.shape[1:])
+    lengths[dim] *= blocks.shape[0]
+    return jnp.moveaxis(blocks, 0, dim).reshape(lengths)
 
 
 def normalize(values):
@@ -55,13 +67,15 @@
     present = jnp.sum(chosen_int, axis=-1) > 0
     user_slot = jnp.sum(chosen_int * all_users[:, None, :], axis=-1)
     picked = kv_cache[user_slot]
-    arrived = lax.all_to_all(
-        jnp.where(present[:, :, None, None], picked, jnp.zeros_like(picked)),
-        "req",
-        split_axis=0,
-        concat_axis=0,
-        tiled=True,
-    )
+    x = jnp.where(present[:, :, None, None], picked, jnp.zeros_like(picked))
+    peers, index = (lax.axis_size("req"), lax.axis_index("req"))
+    blocks = split_up(x, 0, peers)
+    outs = [blocks[index]]
+    for step in range(1, peers):
+        sent = blocks[(index + step) % peers]
+        outs.append(lax.ppermute(sent, "req", [(i, (i + step) % peers) for i in range(peers)]))
+    blocks = jnp.stack(outs)[(index - jnp.arange(peers)) % peers]
+    arrived = joined_along(blocks, 0)
     own_ranks = slot_ranks(owners)
     normed = normalize(candidates.astype(jnp.float32)).astype(jnp.bfloat16)
     projected = jax.nn.silu(jnp.dot(normed, w_in, preferred_element_type=jnp.float32)).astype(

time: 484 us -> 493 us (1.019)
  local copies, waits for them, and re-layouts: 92.8 us -> 122 us
  waiting for transfers between devices: 247 us -> 226 us
    all_to_all x1 -> x0, waiting for transfers between devices: 147 us -> none  [per_device(): lax.all_to_all(jnp.where(present[:, :, None, None], picked, jnp.zeros_lik...]
    ppermute x0 -> x7, waiting for transfers between devices: none -> 77.4 us  [per_device(): lax.ppermute(sent, 'req', [(i, (i + step) % peers) for i in range(peers)])]
    reduce_scatter x1, waiting for transfers between devices: 99.7 us -> 148 us  [per_device(): lax.psum_scatter(partial_out, 'head', scatter_dimension=1, tiled=True)]
    unnamed x21 -> x32, local copies, waits for them, and re-layouts: 11.2 us -> 25.7 us
    ppermute x0 -> x7, starting transfers between devices: none -> 10.1 us  [per_device(): lax.ppermute(sent, 'req', [(i, (i + step) % peers) for i in range(peers)])]
    gather x0 -> x1, local copies, waits for them, and re-layouts: none -> 8.08 us  [per_device(): blocks = jnp.stack(outs)[(index - jnp.arange(peers)) % peers]]
    squeeze x0 -> x1, local copies, waits for them, and re-layouts: none -> 6.27 us  [per_device(): sent = blocks[(index + step) % peers]]
    all_to_all x1 -> x0, starting transfers between devices: 5.04 us -> none  [per_device(): lax.all_to_all(jnp.where(present[:, :, None, None], picked, jnp.zeros_lik...]
  transfers between devices with their start and end apart: 2 -> 8, of which waited for: 2 -> 3; matrix products, arithmetic and copies ran while one was open for 7% -> 10% of each run, Pallas kernels for 0% -> 0%
where the time goes in v1:
time: 493 us; the launch traced here: 490 us
  waiting for transfers between devices  226 us (46%)
  local copies, waits for them, and re-layouts  122 us (25%)
  matrix products  48.4 us (10%)
  other arithmetic  35.2 us (7%)
  loops' own time  22.8 us (5%)
  between operations  14.3 us (3%)
  blocking collectives  10.6 us (2%)
  starting transfers between devices  10.1 us (2%)
    reduce_scatter x1, waiting for transfers between devices, per_device(): lax.psum_scatter(partial_out, 'head', scatter_dimension=1, tiled=True)  148 us
    ppermute x7, waiting for transfers between devices, per_device(): lax.ppermute(sent, 'req', [(i, (i + step) % peers) for i in range(peers)])  77.4 us
    dynamic_update_slice x8, local copies, waits for them, and re-layouts, add_request(): return lax.dynamic_update_slice_in_dim(total, current + mixed, start, 0)  47.1 us
    dot_general x8, matrix products, add_request(): jnp.einsum('hwt,thd->whd', weights, cached[:, :, 1], preferred_element_ty...  27.4 us
    unnamed x32, local copies, waits for them, and re-layouts  25.7 us
    another operation x1, loops' own time, per_device(): attended = lax.fori_loop(0, owners.shape[0], add_request, attended)  22.8 us
    dot_general x1, matrix products, per_device(): jnp.dot(normed, w_in, preferred_element_type=jnp.float32)  15.4 us
    dynamic_slice x16, local copies, waits for them, and re-layouts, add_request(): cached = arrived[source, slot].reshape(-1, local_heads, 2, HD)  14.7 us
  transfers between devices with their start and end apart: 8, of which 3 were waited for; matrix products, arithmetic and copies ran while one was open for 10% of the time, Pallas kernels for 0%

profile of v1, /device:TPU:0, one launch (start us, length us, event | category | flops | bytes accessed | tf_op | source)
XLA Modules:
  0.0 490.0 jit_solution(10615824830760252706)
XLA Ops:
  10.1 10.6 %all-reduce.2 = (s32[64]{0:T(128)S(1)}, s32[64]{0:T(128)S(1)}) all-reduce(s32[64]{0:T(128)S(1)} %bitcast_dynamic-update-slice_fusion.8, s32[64]{0:T(128)S(1)} %dynamic-update-slice.1), channel_id=2, replica_groups=mesh['groups'=2,'req'=8,'head'=2,'rep'=1] {'req'}, use_global_device_ids=true, to_apply=%add | all-reduce | flops 128 | bytes 1024
  21.6 8.0 %gather_fusion = bf16[8,512,1024]{2,1,0:T(8,128)(2,1)} fusion(bf16[8,512,1024]{2,1,0:T(8,128)(2,1)} %param.15, s32[1024]{0:T(1024)S(1)} %pad_clamp_fusion.1), kind=kCustom, calls=%fused_computation | custom fusion | bytes 16777248 | tf_op jit(solution)/shard_map/gather | solution.py:69
  29.7 7.2 %bitcast_select_fusion = bf16[8,1,512,1024]{3,2,1,0:T(8,128)(2,1)} fusion(bf16[8,512,1024]{2,1,0:T(8,128)(2,1)} %gather_fusion, pred[8]{0:T(512)(128)(4,1)S(1)} %broadcast_compare_fusion.1), kind=kLoop, calls=%fused_computation.26 | loop fusion | flops 4194304 | bytes 16777224 | tf_op jit(solution)/shard_map/jit(_where)/select_n | solution.py:70
  36.9 6.3 %constant_dynamic-slice_fusion.1 = (bf16[1,1,512,1024]{3,2,1,0:T(8,128)(2,1)}, bf16[1,1,512,1024]{3,2,1,0:T(8,128)(2,1)}, bf16[1,1,512,1024]{3,2,1,0:T(8,128)(2,...) fusion(bf16[8,1,512,1024]{3,2,1,0:T(8,128)(2,1)} %bitcast_selec, ...), kind=kLoop, calls=%fused_computation.61 | loop fusion | bytes 14680092 | tf_op jit(solution)/shard_map/squeeze | solution.py:75
  44.3 3.5 collective-permute-start.3
  49.9 15.4 %multiply_convert_fusion = bf16[2048,2048]{0,1:T(8,128)(2,1)S(1)} fusion(bf16[1024,2048]{1,0:T(8,128)(2,1)} %param.16, bf16[2048,1024]{1,0:T(8,128)(2,1)S(1)} %copy-done.2, f32[2048]{0:T(1024)S(1)} %add_rsqrt_fusion.1, f32[2048]{0:T(1024)S(1)} %broadcast_multiply_fusion.1), kind=kOutput, calls=%fused_computation.19 | convolution fusion | flops 8619294720 | bytes 16793600 | tf_op jit(solution)/shard_map/dot_general | solution.py:81
  71.7 3.0 copy.62
  77.5 4.3 convert_multiply_fusion.1
  88.6 3.4 collective-permute-start.6
  94.2 66.3 %collective-permute-done.2 = bf16[1,1,512,1024]{3,2,1,0:T(8,128)(2,1)} collective-permute-done((bf16[1,1,512,1024]{3,2,1,0:T(8,128)(2,1)}, bf16[1,1,512,1024]{3,2,1,0:T(8,128)(2,1)}, u32[]{:S(2)}, u32[]{:S(2)}) %collective-permute-start.2) | collective-permute-done | bytes 1048608 | tf_op jit(solution)/shard_map/ppermute | solution.py:76
  168.5 11.1 %collective-permute-done.6 = bf16[1,1,512,1024]{3,2,1,0:T(8,128)(2,1)S(1)} collective-permute-done((bf16[1,1,512,1024]{3,2,1,0:T(8,128)(2,1)S(1)}, bf16[1,1,512,1024]{3,2,1,0:T(8,128)(2,1)S(1)}, u32[]{:S(2)}, u32[]{:S(2)}) %collective-permute-start.6) | collective-permute-done | bytes 1048608 | tf_op jit(solution)/shard_map/ppermute | solution.py:76
  180.6 8.1 %gather_fusion.1 = bf16[8,512,1024]{2,1,0:T(8,128)(2,1)} fusion(bf16[8,512,1024]{2,1,0:T(8,128)(2,1)} %bitcast.25, s32[1024]{0:T(1024)S(1)} %pad_clamp_fusion), kind=kCustom, calls=%fused_computation.1 | custom fusion | bytes 16777248 | tf_op jit(solution)/shard_map/gather | solution.py:77
  188.7 127.0 %while.14 = (s32[]{:T(128)}, f32[2048,4,128]{0,2,1:T(8,128)}, s32[2048]{0:T(1024)S(1)}, s32[8]{0:T(128)S(1)}, bf16[8,1,512,1024]{3,2,0,1:T(8,128)(2,1)}, /*index...) while((s32[]{:T(128)}, f32[2048,4,128]{0,2,1:T(8,128)}, ...), condition=%wide.region_8.9_spmd.clone, body=%wide.region_6.8_spmd.clone.sunk | while | flops 544742400 | bytes 9975023 | solution.py:119
  195.3 3.4 fusion.36
  198.8 5.8 %dynamic_update_slice.9 = f32[2048,4,128]{0,2,1:T(8,128)} dynamic-update-slice(f32[2048,4,128]{0,2,1:T(8,128)} %get-tuple-element.275, f32[512,4,128]{0,2,1:T(8,128)S(1)} %fusion.36, s32[]{:T(128)S(6)} %min.10, s32[]{:T(128)} %constant.141.clone.1..sunk, s32[]{:T(128)} %constant.141.clone.1..sunk) | dynamic-update-slice | bytes 2097156 | tf_op jit(solution)/shard_map/while/body/eval_jaxpr/dynamic_update_slice | solution.py:117
  211.1 3.4 fusion.36
  214.5 6.3 %dynamic_update_slice.9 = f32[2048,4,128]{0,2,1:T(8,128)} dynamic-update-slice(f32[2048,4,128]{0,2,1:T(8,128)} %get-tuple-element.275, f32[512,4,128]{0,2,1:T(8,128)S(1)} %fusion.36, s32[]{:T(128)S(6)} %min.10, s32[]{:T(128)} %constant.141.clone.1..sunk, s32[]{:T(128)} %constant.141.clone.1..sunk) | dynamic-update-slice | bytes 2097156 | tf_op jit(solution)/shard_map/while/body/eval_jaxpr/dynamic_update_slice | solution.py:117
  227.4 3.4 fusion.36
  230.8 6.3 %dynamic_update_slice.9 = f32[2048,4,128]{0,2,1:T(8,128)} dynamic-update-slice(f32[2048,4,128]{0,2,1:T(8,128)} %get-tuple-element.275, f32[512,4,128]{0,2,1:T(8,128)S(1)} %fusion.36, s32[]{:T(128)S(6)} %min.10, s32[]{:T(128)} %constant.141.clone.1..sunk, s32[]{:T(128)} %constant.141.clone.1..sunk) | dynamic-update-slice | bytes 2097156 | tf_op jit(solution)/shard_map/while/body/eval_jaxpr/dynamic_update_slice | solution.py:117
  243.7 3.4 fusion.36
  247.1 6.3 %dynamic_update_slice.9 = f32[2048,4,128]{0,2,1:T(8,128)} dynamic-update-slice(f32[2048,4,128]{0,2,1:T(8,128)} %get-tuple-element.275, f32[512,4,128]{0,2,1:T(8,128)S(1)} %fusion.36, s32[]{:T(128)S(6)} %min.10, s32[]{:T(128)} %constant.141.clone.1..sunk, s32[]{:T(128)} %constant.141.clone.1..sunk) | dynamic-update-slice | bytes 2097156 | tf_op jit(solution)/shard_map/while/body/eval_jaxpr/dynamic_update_slice | solution.py:117
  259.9 3.4 fusion.36
  263.4 6.3 %dynamic_update_slice.9 = f32[2048,4,128]{0,2,1:T(8,128)} dynamic-update-slice(f32[2048,4,128]{0,2,1:T(8,128)} %get-tuple-element.275, f32[512,4,128]{0,2,1:T(8,128)S(1)} %fusion.36, s32[]{:T(128)S(6)} %min.10, s32[]{:T(128)} %constant.141.clone.1..sunk, s32[]{:T(128)} %constant.141.clone.1..sunk) | dynamic-update-slice | bytes 2097156 | tf_op jit(solution)/shard_map/while/body/eval_jaxpr/dynamic_update_slice | solution.py:117
  276.2 3.4 fusion.36
  279.7 6.3 %dynamic_update_slice.9 = f32[2048,4,128]{0,2,1:T(8,128)} dynamic-update-slice(f32[2048,4,128]{0,2,1:T(8,128)} %get-tuple-element.275, f32[512,4,128]{0,2,1:T(8,128)S(1)} %fusion.36, s32[]{:T(128)S(6)} %min.10, s32[]{:T(128)} %constant.141.clone.1..sunk, s32[]{:T(128)} %constant.141.clone.1..sunk) | dynamic-update-slice | bytes 2097156 | tf_op jit(solution)/shard_map/while/body/eval_jaxpr/dynamic_update_slice | solution.py:117
  292.5 3.4 fusion.36
  295.8 5.0 %dynamic_update_slice.9 = f32[2048,4,128]{0,2,1:T(8,128)} dynamic-update-slice(f32[2048,4,128]{0,2,1:T(8,128)} %get-tuple-element.275, f32[512,4,128]{0,2,1:T(8,128)S(1)} %fusion.36, s32[]{:T(128)S(6)} %min.10, s32[]{:T(128)} %constant.141.clone.1..sunk, s32[]{:T(128)} %constant.141.clone.1..sunk) | dynamic-update-slice | bytes 2097156 | tf_op jit(solution)/shard_map/while/body/eval_jaxpr/dynamic_update_slice | solution.py:117
  307.4 3.3 fusion.36
  310.7 5.0 %dynamic_update_slice.9 = f32[2048,4,128]{0,2,1:T(8,128)} dynamic-update-slice(f32[2048,4,128]{0,2,1:T(8,128)} %get-tuple-element.275, f32[512,4,128]{0,2,1:T(8,128)S(1)} %fusion.36, s32[]{:T(128)S(6)} %min.10, s32[]{:T(128)} %constant.141.clone.1..sunk, s32[]{:T(128)} %constant.141.clone.1..sunk) | dynamic-update-slice | bytes 2097156 | tf_op jit(solution)/shard_map/while/body/eval_jaxpr/dynamic_update_slice | solution.py:117
  324.1 5.6 %fusion.29 = f32[2048,1024]{1,0:T(8,128)} fusion(bf16[2048,512]{0,1:T(8,128)(2,1)S(1)} %bitcast.103, bf16[512,1024]{1,0:T(8,128)(2,1)S(1)} %copy-done), kind=kOutput, calls=%fused_computation.78 | convolution fusion | flops 2147483648 | bytes 11534336 | tf_op jit(solution)/shard_map/dot_general | solution.py:125
  329.7 148.5 %reduce-scatter.2.cloned.1.call-done = f32[2048,512]{1,0:T(8,128)} async-done(((f32[2048,1024]{1,0:T(8,128)}), f32[2048,512]{1,0:T(8,128)}) %reduce-scatter.2.cloned.1.call-update) | async-done | bytes 4194320 | tf_op jit(solution)/shard_map/reduce_scatter | solution.py:126
  478.2 4.9 %add_convert_fusion = bf16[2048,512]{1,0:T(8,128)(2,1)} fusion(f32[2048,512]{1,0:T(8,128)} %reduce-scatter.2.cloned.1.call-done, bf16[2048,1024]{1,0:T(8,128)(2,1)} %param.10, s32[]{:T(128)S(6)} %select_n.166), kind=kLoop, calls=%fused_computation.33 | loop fusion | flops 3145728 | bytes 8388612 | tf_op jit(solution)/shard_map/convert_element_type | solution.py:131
  (116 shorter events, 72.1 us)
Async XLA Ops:
  6.5 317.6 %copy-start = (bf16[512,1024]{1,0:T(8,128)(2,1)S(1)}, bf16[512,1024]{1,0:T(8,128)(2,1)}, u32[]{:S(2)}) copy-start(bf16[512,1024]{1,0:T(8,128)(2,1)} %param.17) | copy-start | bytes 3145732
  6.5 471.7 %reduce-scatter.2.cloned.1.call-start = ((), (), s32[]{:S(2)}) async-start(), calls=%async_computation.1 | async-start | bytes 12582912 | tf_op jit(solution)/shard_map/reduce_scatter | solution.py:126
  36.9 11.0 %copy-start.2 = (bf16[2048,1024]{1,0:T(8,128)(2,1)S(1)}, bf16[2048,1024]{1,0:T(8,128)(2,1)}, u32[]{:S(2)}) copy-start(bf16[2048,1024]{1,0:T(8,128)(2,1)} %param.10) | copy-start | bytes 12582916
  43.1 41.0 %collective-permute-start = (bf16[1,1,512,1024]{3,2,1,0:T(8,128)(2,1)}, bf16[1,1,512,1024]{3,2,1,0:T(8,128)(2,1)}, u32[]{:S(2)}, u32[]{:S(2)}) collective-permute-start(bf16[1,1,512,1024]{3,2,1,0:T(8,128)(2,1)} %get-tuple-element.212), channel_id=1, source_target_pairs={{0,2},{2,4},{4,6},{6,8},{8,10},{10,12},{12,14},{14,0},{1,3},{3,5},... | collective-permute-start | bytes 3145736 | tf_op jit(solution)/shard_map/ppermute | solution.py:76
  43.1 45.4 %collective-permute-start.1 = (bf16[1,1,512,1024]{3,2,1,0:T(8,128)(2,1)}, bf16[1,1,512,1024]{3,2,1,0:T(8,128)(2,1)}, u32[]{:S(2)}, u32[]{:S(2)}) collective-permute-start(bf16[1,1,512,1024]{3,2,1,0:T(8,128)(2,1)} %get-tuple-element.211), channel_id=1, source_target_pairs={{0,4},{2,6},{4,8},{6,10},{8,12},{10,14},{12,0},{14,2},{1,5},{3,7},... | collective-permute-start | bytes 3145736 | tf_op jit(solution)/shard_map/ppermute | solution.py:76
  44.0 116.5 %collective-permute-start.2 = (bf16[1,1,512,1024]{3,2,1,0:T(8,128)(2,1)}, bf16[1,1,512,1024]{3,2,1,0:T(8,128)(2,1)}, u32[]{:S(2)}, u32[]{:S(2)}) collective-permute-start(bf16[1,1,512,1024]{3,2,1,0:T(8,128)(2,1)} %get-tuple-element.210), channel_id=1, source_target_pairs={{0,6},{2,8},{4,10},{6,12},{8,14},{10,0},{12,2},{14,4},{1,7},{3,9},... | collective-permute-start | bytes 3145736 | tf_op jit(solution)/shard_map/ppermute | solution.py:76
  44.3 118.5 %collective-permute-start.3 = (bf16[1,1,512,1024]{3,2,1,0:T(8,128)(2,1)}, bf16[1,1,512,1024]{3,2,1,0:T(8,128)(2,1)}, u32[]{:S(2)}, u32[]{:S(2)}) collective-permute-start(bf16[1,1,512,1024]{3,2,1,0:T(8,128)(2,1)} %get-tuple-element.209), channel_id=1, source_target_pairs={{0,8},{2,10},{4,12},{6,14},{8,0},{10,2},{12,4},{14,6},{1,9},{3,11}... | collective-permute-start | bytes 3145736 | tf_op jit(solution)/shard_map/ppermute | solution.py:76
  47.8 117.3 %collective-permute-start.4 = (bf16[1,1,512,1024]{3,2,1,0:T(8,128)(2,1)}, bf16[1,1,512,1024]{3,2,1,0:T(8,128)(2,1)}, u32[]{:S(2)}, u32[]{:S(2)}) collective-permute-start(bf16[1,1,512,1024]{3,2,1,0:T(8,128)(2,1)} %get-tuple-element.208), channel_id=1, source_target_pairs={{0,10},{2,12},{4,14},{6,0},{8,2},{10,4},{12,6},{14,8},{1,11},{3,13... | collective-permute-start | bytes 3145736 | tf_op jit(solution)/shard_map/ppermute | solution.py:76
  65.3 3.8 copy-start.3
  77.5 6.6 %copy-start.5 = (bf16[1,1,512,1024]{3,2,1,0:T(8,128)(2,1)S(1)}, bf16[1,1,512,1024]{3,2,1,0:T(8,128)(2,1)}, u32[]{:S(2)}) copy-start(bf16[1,1,512,1024]{3,2,1,0:T(8,128)(2,1)} %get-tuple-element.207) | copy-start | bytes 3145732
  77.5 11.0 %copy-start.4 = (bf16[1,1,512,1024]{3,2,1,0:T(8,128)(2,1)S(1)}, bf16[1,1,512,1024]{3,2,1,0:T(8,128)(2,1)}, u32[]{:S(2)}) copy-start(bf16[1,1,512,1024]{3,2,1,0:T(8,128)(2,1)} %get-tuple-element.206) | copy-start | bytes 3145732
  84.2 83.2 %collective-permute-start.5 = (bf16[1,1,512,1024]{3,2,1,0:T(8,128)(2,1)S(1)}, bf16[1,1,512,1024]{3,2,1,0:T(8,128)(2,1)S(1)}, u32[]{:S(2)}, u32[]{:S(2)}) collective-permute-start(bf16[1,1,512,1024]{3,2,1,0:T(8,128)(2,1)S(1)} %copy-done.5), channel_id=1, source_target_pairs={{0,12},{2,14},{4,0},{6,2},{8,4},{10,6},{12,8},{14,10},{1,13},{3,15... | collective-permute-start | bytes 3145736 | tf_op jit(solution)/shard_map/ppermute | solution.py:76
  88.6 91.0 %collective-permute-start.6 = (bf16[1,1,512,1024]{3,2,1,0:T(8,128)(2,1)S(1)}, bf16[1,1,512,1024]{3,2,1,0:T(8,128)(2,1)S(1)}, u32[]{:S(2)}, u32[]{:S(2)}) collective-permute-start(bf16[1,1,512,1024]{3,2,1,0:T(8,128)(2,1)S(1)} %copy-done.4), channel_id=1, source_target_pairs={{0,14},{2,0},{4,2},{6,4},{8,6},{10,8},{12,10},{14,12},{1,15},{3,1}... | collective-permute-start | bytes 3145736 | tf_op jit(solution)/shard_map/ppermute | solution.py:76
  180.6 8.1 %copy-start.6 = (s32[1,2048]{1,0:T(1,128)S(1)}, s32[1,2048]{1,0:T(1,128)}, u32[]{:S(2)}) copy-start(s32[1,2048]{1,0:T(1,128)} %param.11) | copy-start | bytes 24580
  180.6 8.1 %copy-start.7 = (s32[8,1]{0,1:T(1,128)S(1)}, s32[8,1]{0,1:T(1,128)}, u32[]{:S(2)}) copy-start(s32[8,1]{0,1:T(1,128)} %param.12) | copy-start | bytes 100
  180.6 8.1 %copy-start.8 = (s32[1,8]{1,0:T(1,128)S(1)}, s32[1,8]{1,0:T(1,128)}, u32[]{:S(2)}) copy-start(s32[1,8]{1,0:T(1,128)} %param.14) | copy-start | bytes 100
  318.2 3.5 copy-start.1
Sparse Core Ops, SparseCore 0:
  329.9 148.3 reduce-scatter.1
